TPU v7x, 32 devices: a whole 2x2x4 slice. The times are simulated.
32 devices in a mesh: pb: 4 (over y, core), ka: 8 (over z, x).
Axes of the slice: x: 2, y: 2, z: 4, core: 2. Of those that a mesh axis runs over, the one named last changes fastest.
Arguments:
- queries: float32 [2048, 128], P('pb'), may hold values from -36 to 36
- cache_keys: float32 [65536, 128], P('ka'), may hold values from -4 to 4
- cache_values: float32 [65536, 128], P('ka'), may hold values from -6 to 6
- kept_index: int32 [4096], P('ka'), may hold values from 0 to 65535, as said below
Outputs:
- fitted: float32 [4096, 128], P('ka')
Inputs may be any that keep to these rules, and one draw needn't show every extreme that they name: `kept_index`: Increasing; the t-th kept index lies among the cache rows t * (16) to (t + 1) * 16 - 1, so the kept keys of a device are rows of its own block of the cache.
All inputs are finite; a program needn't handle non-finite values.
Results may differ from a plain program's by a relative error of at most 0.0003.
Values sent between devices are 32-bit elements; how exact they have to be, the bound alone decides.
A program may use at most 128 MiB of HBM per device.

v0:
```python
import math
import jax
import jax.numpy as jnp
from jax import lax
from jax.sharding import PartitionSpec as P

ITERS = 2
ridge_weight = 0.01
highest = lax.Precision.HIGHEST


def contract(left_side, right_side, left_dim, right_dim):
    return lax.dot_general(
        left_side,
        right_side,
        (((left_dim,), (right_dim,)), ((), ())),
        precision=highest,
        preferred_element_type=jnp.float32,
    )


def column_sums(left_side, right_side):
    return jnp.sum(left_side * right_side, axis=0, keepdims=True)


def padded(rows, *tail):
    used = sum((part.shape[0] for part in tail))
    fill = jnp.zeros((-used % 8, rows.shape[1]), rows.dtype)
    return jnp.concatenate((rows,) + tail + (fill,), axis=0)


def shards(queries, cache_keys, cache_values, kept_index):
    query_rows, head_width = queries.shape
    inverse_root = 1.0 / math.sqrt(head_width)
    cache_rows = cache_keys.shape[0]
    block_size = min(1024, cache_rows)
    blocks = cache_rows // block_size
    local_kept = kept_index - lax.axis_index("ka") * cache_rows
    kept_keys = jnp.take(cache_keys, local_kept, axis=0)
    kept_scores = contract(queries, kept_keys, 1, 1) * inverse_root
    kept_top = jnp.max(kept_scores, axis=1)
    kept_exponent = jnp.exp(kept_scores - kept_top[:, None])
    kept_total = jnp.sum(kept_exponent, axis=1)

    def step(block_number, state):
        top, total, numerator = state
        start = block_number * block_size
        keys_block = lax.dynamic_slice_in_dim(cache_keys, start, block_size, axis=0)
        values_block = lax.dynamic_slice_in_dim(cache_values, start, block_size, axis=0)
        scores = contract(queries, keys_block, 1, 1) * inverse_root
        top_next = jnp.maximum(top, jnp.max(scores, axis=1))
        factor = jnp.exp(top - top_next)
        exponent = jnp.exp(scores - top_next[:, None])
        return (
            top_next,
            total * factor + jnp.sum(exponent, axis=1),
            numerator * factor[:, None] + contract(exponent, values_block, 1, 0),
        )

    top, total, numerator = lax.fori_loop(
        0,
        blocks,
        step,
        (
            jnp.full((query_rows,), -jnp.inf, jnp.float32),
            jnp.zeros((query_rows,), jnp.float32),
            jnp.zeros((query_rows, head_width), jnp.float32),
        ),
    )
    stats = jnp.concatenate((top, total, kept_top, kept_total)).reshape(-1, head_width)
    gathered = lax.all_gather(padded(numerator, stats), "ka")
    shares = gathered.shape[0]
    gathered_stats = gathered[:, query_rows : query_rows + stats.shape[0]]
    gathered_stats = gathered_stats.reshape(shares, 4, query_rows)
    factors = jnp.exp(gathered_stats[:, 0] - jnp.max(gathered_stats[:, 0], axis=0))
    target_total = jnp.sum(gathered_stats[:, 1] * factors, axis=0)
    target = jnp.sum(gathered[:, :query_rows] * factors[:, :, None], axis=0)
    target = target / target_total[:, None]
    kept_joint = jnp.max(gathered_stats[:, 2], axis=0)
    joint_total = jnp.sum(gathered_stats[:, 3] * jnp.exp(gathered_stats[:, 2] - kept_joint), axis=0)
    weights = kept_exponent * (jnp.exp(kept_top - kept_joint) / joint_total)[:, None]
    residual = lax.psum(contract(weights, target, 0, 0), "pb")
    kept_rows = residual.shape[0]
    fitted = jnp.zeros_like(residual)
    direction = residual
    updates = None
    norm_now = None
    length_now = None
    for iteration in range(ITERS):
        final_turn = iteration + 1 == ITERS
        forward = contract(weights, residual, 1, 0)
        if iteration == 0:
            summed = lax.psum(padded(forward, column_sums(residual, residual)), "ka")
            updates = summed[:query_rows]
            norm_now = summed[query_rows : query_rows + 1]
            length_now = norm_now
        else:
            summed = lax.psum(
                padded(forward, column_sums(residual, residual), column_sums(residual, direction)),
                "ka",
            )
            norm_next = summed[query_rows : query_rows + 1]
            crossed = summed[query_rows + 1 : query_rows + 2]
            ratio = norm_next / norm_now
            direction = residual + ratio * direction
            updates = summed[:query_rows] + ratio * updates
            length_now = norm_next + 2.0 * ratio * crossed + ratio * ratio * length_now
            norm_now = norm_next
        energy = column_sums(updates, updates)
        if final_turn:
            energy = lax.psum(energy, "pb")
            fitted = fitted + norm_now / (energy + ridge_weight * length_now) * direction
        else:
            summed = lax.psum(padded(contract(weights, updates, 0, 0), energy), "pb")
            operator_image = summed[:kept_rows] + ridge_weight * direction
            energy = summed[kept_rows : kept_rows + 1]
            step_length = norm_now / (energy + ridge_weight * length_now)
            fitted = fitted + step_length * direction
            residual = residual - step_length * operator_image
    return fitted


def solution(mesh):
    in_specs = (P("pb", None), P("ka", None), P("ka", None), P("ka"))
    out_specs = P("ka", None)
    return jax.shard_map(shards, mesh=mesh, in_specs=in_specs, out_specs=out_specs, check_vma=False)
```

profile of v0, /device:TPU:0, one launch (start us, length us, event | category | flops | bytes accessed | tf_op | source)
XLA Modules:
  0.0 368.8 jit_solution(18405595993020933643)
XLA Ops:
  7.3 3.2 gather_fusion
  10.5 64.1 %while.18 = (s32[]{:T(128)}, f32[512]{0:T(512)S(1)}, f32[512]{0:T(512)S(1)}, f32[512,128]{1,0:T(8,128)S(1)}, f32[8192,128]{1,0:T(8,128)}, /*index=5*/f32[512,128...) while((s32[]{:T(128)}, f32[512]{0:T(512)S(1)}, ...), condition=%wide.region_4.5_spmd.clone, body=%wide.region_1.0_spmd.clone.sunk | while | flops 1614481920 | bytes 8159415 | solution.py:60
  10.5 2.9 multiply_reduce_fusion.6
  13.9 4.6 %fusion.62 = f32[512,128]{1,0:T(8,128)S(1)} fusion(f32[1024,512]{1,0:T(8,128)S(1)} %get-tuple-element.239, f32[512]{0:T(512)S(1)} %select_maximum_fusion.2, f32[8192,128]{1,0:T(8,128)} %get-tuple-element.270, s32[]{:T(128)S(6)} %select_n.27, f32[512,128]{1,0:T(8,128)S(1)} %get-tuple-element.256, f32[512]{0:T(512)S(1)} %get-tuple-element.241, ...), kind=kOutput, calls=%fused_computation.5.clone.1 | convolution fusion | flops 806551552 | bytes 3149829 | tf_op jit(solution)/shard_map/while/body/eval_jaxpr/dot_general | solution.py:13
  18.6 2.9 multiply_reduce_fusion.6
  21.9 4.6 %fusion.62 = f32[512,128]{1,0:T(8,128)S(1)} fusion(f32[1024,512]{1,0:T(8,128)S(1)} %get-tuple-element.239, f32[512]{0:T(512)S(1)} %select_maximum_fusion.2, f32[8192,128]{1,0:T(8,128)} %get-tuple-element.270, s32[]{:T(128)S(6)} %select_n.27, f32[512,128]{1,0:T(8,128)S(1)} %get-tuple-element.256, f32[512]{0:T(512)S(1)} %get-tuple-element.241, ...), kind=kOutput, calls=%fused_computation.5.clone.1 | convolution fusion | flops 806551552 | bytes 3149829 | tf_op jit(solution)/shard_map/while/body/eval_jaxpr/dot_general | solution.py:13
  26.6 2.9 multiply_reduce_fusion.6
  29.9 4.6 %fusion.62 = f32[512,128]{1,0:T(8,128)S(1)} fusion(f32[1024,512]{1,0:T(8,128)S(1)} %get-tuple-element.239, f32[512]{0:T(512)S(1)} %select_maximum_fusion.2, f32[8192,128]{1,0:T(8,128)} %get-tuple-element.270, s32[]{:T(128)S(6)} %select_n.27, f32[512,128]{1,0:T(8,128)S(1)} %get-tuple-element.256, f32[512]{0:T(512)S(1)} %get-tuple-element.241, ...), kind=kOutput, calls=%fused_computation.5.clone.1 | convolution fusion | flops 806551552 | bytes 3149829 | tf_op jit(solution)/shard_map/while/body/eval_jaxpr/dot_general | solution.py:13
  34.6 2.9 multiply_reduce_fusion.6
  37.9 4.6 %fusion.62 = f32[512,128]{1,0:T(8,128)S(1)} fusion(f32[1024,512]{1,0:T(8,128)S(1)} %get-tuple-element.239, f32[512]{0:T(512)S(1)} %select_maximum_fusion.2, f32[8192,128]{1,0:T(8,128)} %get-tuple-element.270, s32[]{:T(128)S(6)} %select_n.27, f32[512,128]{1,0:T(8,128)S(1)} %get-tuple-element.256, f32[512]{0:T(512)S(1)} %get-tuple-element.241, ...), kind=kOutput, calls=%fused_computation.5.clone.1 | convolution fusion | flops 806551552 | bytes 3149829 | tf_op jit(solution)/shard_map/while/body/eval_jaxpr/dot_general | solution.py:13
  42.6 2.9 multiply_reduce_fusion.6
  46.0 4.6 %fusion.62 = f32[512,128]{1,0:T(8,128)S(1)} fusion(f32[1024,512]{1,0:T(8,128)S(1)} %get-tuple-element.239, f32[512]{0:T(512)S(1)} %select_maximum_fusion.2, f32[8192,128]{1,0:T(8,128)} %get-tuple-element.270, s32[]{:T(128)S(6)} %select_n.27, f32[512,128]{1,0:T(8,128)S(1)} %get-tuple-element.256, f32[512]{0:T(512)S(1)} %get-tuple-element.241, ...), kind=kOutput, calls=%fused_computation.5.clone.1 | convolution fusion | flops 806551552 | bytes 3149829 | tf_op jit(solution)/shard_map/while/body/eval_jaxpr/dot_general | solution.py:13
  50.6 2.9 multiply_reduce_fusion.6
  54.0 4.6 %fusion.62 = f32[512,128]{1,0:T(8,128)S(1)} fusion(f32[1024,512]{1,0:T(8,128)S(1)} %get-tuple-element.239, f32[512]{0:T(512)S(1)} %select_maximum_fusion.2, f32[8192,128]{1,0:T(8,128)} %get-tuple-element.270, s32[]{:T(128)S(6)} %select_n.27, f32[512,128]{1,0:T(8,128)S(1)} %get-tuple-element.256, f32[512]{0:T(512)S(1)} %get-tuple-element.241, ...), kind=kOutput, calls=%fused_computation.5.clone.1 | convolution fusion | flops 806551552 | bytes 3149829 | tf_op jit(solution)/shard_map/while/body/eval_jaxpr/dot_general | solution.py:13
  58.6 2.9 multiply_reduce_fusion.6
  62.0 4.6 %fusion.62 = f32[512,128]{1,0:T(8,128)S(1)} fusion(f32[1024,512]{1,0:T(8,128)S(1)} %get-tuple-element.239, f32[512]{0:T(512)S(1)} %select_maximum_fusion.2, f32[8192,128]{1,0:T(8,128)} %get-tuple-element.270, s32[]{:T(128)S(6)} %select_n.27, f32[512,128]{1,0:T(8,128)S(1)} %get-tuple-element.256, f32[512]{0:T(512)S(1)} %get-tuple-element.241, ...), kind=kOutput, calls=%fused_computation.5.clone.1 | convolution fusion | flops 806551552 | bytes 3149829 | tf_op jit(solution)/shard_map/while/body/eval_jaxpr/dot_general | solution.py:13
  66.7 2.9 multiply_reduce_fusion.6
  70.0 4.6 %fusion.62 = f32[512,128]{1,0:T(8,128)S(1)} fusion(f32[1024,512]{1,0:T(8,128)S(1)} %get-tuple-element.239, f32[512]{0:T(512)S(1)} %select_maximum_fusion.2, f32[8192,128]{1,0:T(8,128)} %get-tuple-element.270, s32[]{:T(128)S(6)} %select_n.27, f32[512,128]{1,0:T(8,128)S(1)} %get-tuple-element.256, f32[512]{0:T(512)S(1)} %get-tuple-element.241, ...), kind=kOutput, calls=%fused_computation.5.clone.1 | convolution fusion | flops 806551552 | bytes 3149829 | tf_op jit(solution)/shard_map/while/body/eval_jaxpr/dot_general | solution.py:13
  77.9 52.8 %all-gather.3.cloned.1.call-done = f32[4224,128]{1,0:T(8,128)} async-done(((f32[528,128]{1,0:T(8,128)}), f32[4224,128]{1,0:T(8,128)}) %all-gather.3.cloned.1.call-update) | async-done | bytes 2162704 | tf_op jit(solution)/shard_map/all_gather | solution.py:71
  135.6 30.5 %all-reduce.5.cloned.1.call-done = f32[512,128]{1,0:T(8,128)} async-done(((f32[512,128]{1,0:T(8,128)}), f32[512,128]{1,0:T(8,128)}) %all-reduce.5.cloned.1.call-update) | async-done | bytes 262160 | tf_op jit(solution)/shard_map/psum | solution.py:82
  170.8 70.6 %all-reduce.7.cloned.1.call-done = f32[520,128]{1,0:T(8,128)} async-done(((f32[520,128]{1,0:T(8,128)}), f32[520,128]{1,0:T(8,128)}) %all-reduce.7.cloned.1.call-update) | async-done | bytes 266256 | tf_op jit(solution)/shard_map/psum | solution.py:93
  245.7 30.5 %all-reduce.9.cloned.1.call-done = f32[520,128]{1,0:T(8,128)} async-done(((f32[520,128]{1,0:T(8,128)}), f32[520,128]{1,0:T(8,128)}) %all-reduce.9.cloned.1.call-update) | async-done | bytes 266256 | tf_op jit(solution)/shard_map/psum | solution.py:114
  281.6 71.7 %all-reduce.11.cloned.1.call-done = f32[520,128]{1,0:T(8,128)} async-done(((f32[520,128]{1,0:T(8,128)}), f32[520,128]{1,0:T(8,128)}) %all-reduce.11.cloned.1.call-update) | async-done | bytes 266256 | tf_op jit(solution)/shard_map/psum | solution.py:98
  355.0 5.7 %psum.39 = f32[1,128]{1,0:T(1,128)S(1)} all-reduce(f32[1,128]{1,0:T(1,128)S(1)} %bitcast.57), channel_id=1, replica_groups=mesh['pb'=4,'ka'=8] {'pb'}, use_global_device_ids=true, to_apply=%region_20.21 | all-reduce | flops 128 | bytes 1024 | tf_op jit(solution)/shard_map/psum | solution.py:111
  (83 shorter events, 29.9 us)
Async XLA Ops:
  6.5 4.0 %copy-start = (f32[512,128]{1,0:T(8,128)S(1)}, f32[512,128]{1,0:T(8,128)}, u32[]{:S(2)}) copy-start(f32[512,128]{1,0:T(8,128)} %param.6) | copy-start | bytes 786436
  6.5 124.1 %all-gather.3.cloned.1.call-start = ((), (), s32[]{:S(2)}) async-start(), calls=%async_computation.4 | async-start | bytes 2433024 | tf_op jit(solution)/shard_map/all_gather | solution.py:71
  77.9 88.2 %all-reduce.5.cloned.1.call-start = ((), (), s32[]{:S(2)}) async-start(), calls=%async_computation | async-start | bytes 524288 | tf_op jit(solution)/shard_map/psum | solution.py:82
  135.5 106.0 %all-reduce.7.cloned.1.call-start = ((), (), s32[]{:S(2)}) async-start(), calls=%async_computation.1 | async-start | bytes 532480 | tf_op jit(solution)/shard_map/psum | solution.py:93
  169.9 107.0 %copy-start.1 = (f32[512,128]{1,0:T(8,128)S(1)}, f32[512,128]{1,0:T(8,128)}, u32[]{:S(2)}) copy-start(f32[512,128]{1,0:T(8,128)} %all-reduce.5.cloned.1.call-done) | copy-start | bytes 786436
  170.8 105.4 %all-reduce.9.cloned.1.call-start = ((), (), s32[]{:S(2)}) async-start(), calls=%async_computation.2 | async-start | bytes 532480 | tf_op jit(solution)/shard_map/psum | solution.py:114
  241.5 34.7 %copy-start.2 = (f32[520,128]{1,0:T(8,128)S(1)}, f32[520,128]{1,0:T(8,128)}, u32[]{:S(2)}) copy-start(f32[520,128]{1,0:T(8,128)} %all-reduce.7.cloned.1.call-done) | copy-start | bytes 798724
  245.4 107.9 %all-reduce.11.cloned.1.call-start = ((), (), s32[]{:S(2)}) async-start(), calls=%async_computation.3 | async-start | bytes 532480 | tf_op jit(solution)/shard_map/psum | solution.py:98
  276.2 85.3 %copy-start.3 = (f32[520,128]{1,0:T(8,128)S(1)}, f32[520,128]{1,0:T(8,128)}, u32[]{:S(2)}) copy-start(f32[520,128]{1,0:T(8,128)} %all-reduce.9.cloned.1.call-done) | copy-start | bytes 798724
Sparse Core Ops, SparseCore 0:
  78.0 52.6 all-gather.2
  135.6 30.4 all-reduce.4
  170.9 70.5 all-reduce.6
  245.5 30.6 all-reduce.8
  281.7 71.5 all-reduce.10
where the time goes:
time: 370 us; the launch traced here: 369 us
  waiting for transfers between devices  256 us (69%)
  matrix products  70.8 us (19%)
  other arithmetic  16.1 us (4%)
  between operations  13.2 us (4%)
  local copies, waits for them, and re-layouts  6.21 us (2%)
  blocking collectives  5.66 us (2%)
    psum x1, waiting for transfers between devices, shards(): lax.psum(padded(forward, column_sums(residual, residual), column_sums(res...  71.7 us
    dot_general x21, matrix products, contract(): lax.dot_general(left_side, right_side, (((left_dim,), (right_dim,)), ((),...  70.8 us
    psum x1, waiting for transfers between devices, shards(): summed = lax.psum(padded(forward, column_sums(residual, residual)), 'ka')  70.6 us
    all_gather x1, waiting for transfers between devices, shards(): gathered = lax.all_gather(padded(numerator, stats), 'ka')  52.8 us
    psum x1, waiting for transfers between devices, shards(): residual = lax.psum(contract(weights, target, 0, 0), 'pb')  30.5 us
    psum x1, waiting for transfers between devices, shards(): summed = lax.psum(padded(contract(weights, updates, 0, 0), energy), 'pb')  30.5 us
  transfers between devices with their start and end apart: 5, of which 5 were waited for; matrix products, arithmetic and copies ran while one was open for 0% of the time, Pallas kernels for 0%

commit v1 on v0

--- a/solution.py
+++ b/solution.py
@@ -79,7 +79,7 @@
     kept_joint = jnp.max(gathered_stats[:, 2], axis=0)
     joint_total = jnp.sum(gathered_stats[:, 3] * jnp.exp(gathered_stats[:, 2] - kept_joint), axis=0)
     weights = kept_exponent * (jnp.exp(kept_top - kept_joint) / joint_total)[:, None]
-    residual = lax.psum(contract(weights, target, 0, 0), "pb")
+    residual = jnp.sum(lax.all_gather(contract(weights, target, 0, 0), "pb"), axis=0)
     kept_rows = residual.shape[0]
     fitted = jnp.zeros_like(residual)
     direction = residual

time: 370 us -> 354 us (0.957)
  waiting for transfers between devices: 256 us -> 241 us
    psum x1 -> x0, waiting for transfers between devices: 30.5 us -> none  [shards(): residual = lax.psum(contract(weights, target, 0, 0), 'pb')]
    all_gather x0 -> x1, waiting for transfers between devices: none -> 15.3 us  [shards(): lax.all_gather(contract(weights, target, 0, 0), 'pb')]
where the time goes in v1:
time: 354 us; the launch traced here: 353 us
  waiting for transfers between devices  241 us (68%)
  matrix products  69.8 us (20%)
  other arithmetic  16.4 us (5%)
  between operations  13.2 us (4%)
  local copies, waits for them, and re-layouts  6.21 us (2%)
  blocking collectives  5.66 us (2%)
    psum x1, waiting for transfers between devices, shards(): lax.psum(padded(forward, column_sums(residual, residual), column_sums(res...  71.6 us
    psum x1, waiting for transfers between devices, shards(): summed = lax.psum(padded(forward, column_sums(residual, residual)), 'ka')  70.7 us
    dot_general x21, matrix products, contract(): lax.dot_general(left_side, right_side, (((left_dim,), (right_dim,)), ((),...  69.8 us
    all_gather x1, waiting for transfers between devices, shards(): gathered = lax.all_gather(padded(numerator, stats), 'ka')  52.8 us
    psum x1, waiting for transfers between devices, shards(): summed = lax.psum(padded(contract(weights, updates, 0, 0), energy), 'pb')  30.4 us
    all_gather x1, waiting for transfers between devices, shards(): lax.all_gather(contract(weights, target, 0, 0), 'pb')  15.3 us
  transfers between devices with their start and end apart: 5, of which 5 were waited for; matrix products, arithmetic and copies ran while one was open for 0% of the time, Pallas kernels for 0%

profile of v1, /device:TPU:0, one launch (start us, length us, event | category | flops | bytes accessed | tf_op | source)
XLA Modules:
  0.0 352.9 jit_solution(11141588093737930138)
XLA Ops:
  7.3 3.2 gather_fusion
  10.5 64.1 %while.18 = (s32[]{:T(128)}, f32[512]{0:T(512)S(1)}, f32[512]{0:T(512)S(1)}, f32[512,128]{1,0:T(8,128)S(1)}, f32[8192,128]{1,0:T(8,128)}, /*index=5*/f32[512,128...) while((s32[]{:T(128)}, f32[512]{0:T(512)S(1)}, ...), condition=%wide.region_4.5_spmd.clone, body=%wide.region_1.0_spmd.clone.sunk | while | flops 1614481920 | bytes 8159415 | solution.py:60
  10.5 2.9 multiply_reduce_fusion.6
  13.9 4.6 %fusion.62 = f32[512,128]{1,0:T(8,128)S(1)} fusion(f32[1024,512]{1,0:T(8,128)S(1)} %get-tuple-element.239, f32[512]{0:T(512)S(1)} %select_maximum_fusion.2, f32[8192,128]{1,0:T(8,128)} %get-tuple-element.270, s32[]{:T(128)S(6)} %select_n.27, f32[512,128]{1,0:T(8,128)S(1)} %get-tuple-element.256, f32[512]{0:T(512)S(1)} %get-tuple-element.241, ...), kind=kOutput, calls=%fused_computation.5.clone.1 | convolution fusion | flops 806551552 | bytes 3149829 | tf_op jit(solution)/shard_map/while/body/eval_jaxpr/dot_general | solution.py:13
  18.6 2.9 multiply_reduce_fusion.6
  21.9 4.6 %fusion.62 = f32[512,128]{1,0:T(8,128)S(1)} fusion(f32[1024,512]{1,0:T(8,128)S(1)} %get-tuple-element.239, f32[512]{0:T(512)S(1)} %select_maximum_fusion.2, f32[8192,128]{1,0:T(8,128)} %get-tuple-element.270, s32[]{:T(128)S(6)} %select_n.27, f32[512,128]{1,0:T(8,128)S(1)} %get-tuple-element.256, f32[512]{0:T(512)S(1)} %get-tuple-element.241, ...), kind=kOutput, calls=%fused_computation.5.clone.1 | convolution fusion | flops 806551552 | bytes 3149829 | tf_op jit(solution)/shard_map/while/body/eval_jaxpr/dot_general | solution.py:13
  26.6 2.9 multiply_reduce_fusion.6
  29.9 4.6 %fusion.62 = f32[512,128]{1,0:T(8,128)S(1)} fusion(f32[1024,512]{1,0:T(8,128)S(1)} %get-tuple-element.239, f32[512]{0:T(512)S(1)} %select_maximum_fusion.2, f32[8192,128]{1,0:T(8,128)} %get-tuple-element.270, s32[]{:T(128)S(6)} %select_n.27, f32[512,128]{1,0:T(8,128)S(1)} %get-tuple-element.256, f32[512]{0:T(512)S(1)} %get-tuple-element.241, ...), kind=kOutput, calls=%fused_computation.5.clone.1 | convolution fusion | flops 806551552 | bytes 3149829 | tf_op jit(solution)/shard_map/while/body/eval_jaxpr/dot_general | solution.py:13
  34.6 2.9 multiply_reduce_fusion.6
  37.9 4.6 %fusion.62 = f32[512,128]{1,0:T(8,128)S(1)} fusion(f32[1024,512]{1,0:T(8,128)S(1)} %get-tuple-element.239, f32[512]{0:T(512)S(1)} %select_maximum_fusion.2, f32[8192,128]{1,0:T(8,128)} %get-tuple-element.270, s32[]{:T(128)S(6)} %select_n.27, f32[512,128]{1,0:T(8,128)S(1)} %get-tuple-element.256, f32[512]{0:T(512)S(1)} %get-tuple-element.241, ...), kind=kOutput, calls=%fused_computation.5.clone.1 | convolution fusion | flops 806551552 | bytes 3149829 | tf_op jit(solution)/shard_map/while/body/eval_jaxpr/dot_general | solution.py:13
  42.6 2.9 multiply_reduce_fusion.6
  46.0 4.6 %fusion.62 = f32[512,128]{1,0:T(8,128)S(1)} fusion(f32[1024,512]{1,0:T(8,128)S(1)} %get-tuple-element.239, f32[512]{0:T(512)S(1)} %select_maximum_fusion.2, f32[8192,128]{1,0:T(8,128)} %get-tuple-element.270, s32[]{:T(128)S(6)} %select_n.27, f32[512,128]{1,0:T(8,128)S(1)} %get-tuple-element.256, f32[512]{0:T(512)S(1)} %get-tuple-element.241, ...), kind=kOutput, calls=%fused_computation.5.clone.1 | convolution fusion | flops 806551552 | bytes 3149829 | tf_op jit(solution)/shard_map/while/body/eval_jaxpr/dot_general | solution.py:13
  50.6 2.9 multiply_reduce_fusion.6
  54.0 4.6 %fusion.62 = f32[512,128]{1,0:T(8,128)S(1)} fusion(f32[1024,512]{1,0:T(8,128)S(1)} %get-tuple-element.239, f32[512]{0:T(512)S(1)} %select_maximum_fusion.2, f32[8192,128]{1,0:T(8,128)} %get-tuple-element.270, s32[]{:T(128)S(6)} %select_n.27, f32[512,128]{1,0:T(8,128)S(1)} %get-tuple-element.256, f32[512]{0:T(512)S(1)} %get-tuple-element.241, ...), kind=kOutput, calls=%fused_computation.5.clone.1 | convolution fusion | flops 806551552 | bytes 3149829 | tf_op jit(solution)/shard_map/while/body/eval_jaxpr/dot_general | solution.py:13
  58.6 2.9 multiply_reduce_fusion.6
  62.0 4.6 %fusion.62 = f32[512,128]{1,0:T(8,128)S(1)} fusion(f32[1024,512]{1,0:T(8,128)S(1)} %get-tuple-element.239, f32[512]{0:T(512)S(1)} %select_maximum_fusion.2, f32[8192,128]{1,0:T(8,128)} %get-tuple-element.270, s32[]{:T(128)S(6)} %select_n.27, f32[512,128]{1,0:T(8,128)S(1)} %get-tuple-element.256, f32[512]{0:T(512)S(1)} %get-tuple-element.241, ...), kind=kOutput, calls=%fused_computation.5.clone.1 | convolution fusion | flops 806551552 | bytes 3149829 | tf_op jit(solution)/shard_map/while/body/eval_jaxpr/dot_general | solution.py:13
  66.7 2.9 multiply_reduce_fusion.6
  70.0 4.6 %fusion.62 = f32[512,128]{1,0:T(8,128)S(1)} fusion(f32[1024,512]{1,0:T(8,128)S(1)} %get-tuple-element.239, f32[512]{0:T(512)S(1)} %select_maximum_fusion.2, f32[8192,128]{1,0:T(8,128)} %get-tuple-element.270, s32[]{:T(128)S(6)} %select_n.27, f32[512,128]{1,0:T(8,128)S(1)} %get-tuple-element.256, f32[512]{0:T(512)S(1)} %get-tuple-element.241, ...), kind=kOutput, calls=%fused_computation.5.clone.1 | convolution fusion | flops 806551552 | bytes 3149829 | tf_op jit(solution)/shard_map/while/body/eval_jaxpr/dot_general | solution.py:13
  77.9 52.8 %all-gather.5.cloned.1.call-done = f32[4224,128]{1,0:T(8,128)} async-done(((f32[528,128]{1,0:T(8,128)}), f32[4224,128]{1,0:T(8,128)}) %all-gather.5.cloned.1.call-update) | async-done | bytes 2162704 | tf_op jit(solution)/shard_map/all_gather | solution.py:71
  135.6 15.3 %all-gather.7.cloned.1.call-done = f32[2048,128]{1,0:T(8,128)} async-done(((f32[512,128]{1,0:T(8,128)}), f32[2048,128]{1,0:T(8,128)}) %all-gather.7.cloned.1.call-update) | async-done | bytes 1048592 | tf_op jit(solution)/shard_map/all_gather | solution.py:82
  155.0 70.7 %all-reduce.4.cloned.1.call-done = f32[520,128]{1,0:T(8,128)} async-done(((f32[520,128]{1,0:T(8,128)}), f32[520,128]{1,0:T(8,128)}) %all-reduce.4.cloned.1.call-update) | async-done | bytes 266256 | tf_op jit(solution)/shard_map/psum | solution.py:93
  229.9 30.4 %all-reduce.6.cloned.1.call-done = f32[520,128]{1,0:T(8,128)} async-done(((f32[520,128]{1,0:T(8,128)}), f32[520,128]{1,0:T(8,128)}) %all-reduce.6.cloned.1.call-update) | async-done | bytes 266256 | tf_op jit(solution)/shard_map/psum | solution.py:114
  265.8 71.6 %all-reduce.8.cloned.1.call-done = f32[520,128]{1,0:T(8,128)} async-done(((f32[520,128]{1,0:T(8,128)}), f32[520,128]{1,0:T(8,128)}) %all-reduce.8.cloned.1.call-update) | async-done | bytes 266256 | tf_op jit(solution)/shard_map/psum | solution.py:98
  339.1 5.7 %psum.31 = f32[1,128]{1,0:T(1,128)S(1)} all-reduce(f32[1,128]{1,0:T(1,128)S(1)} %bitcast.59), channel_id=1, replica_groups=mesh['pb'=4,'ka'=8] {'pb'}, use_global_device_ids=true, to_apply=%region_20.21 | all-reduce | flops 128 | bytes 1024 | tf_op jit(solution)/shard_map/psum | solution.py:111
  (82 shorter events, 29.3 us)
Async XLA Ops:
  6.5 4.0 %copy-start = (f32[512,128]{1,0:T(8,128)S(1)}, f32[512,128]{1,0:T(8,128)}, u32[]{:S(2)}) copy-start(f32[512,128]{1,0:T(8,128)} %param.6) | copy-start | bytes 786436
  6.5 124.1 %all-gather.5.cloned.1.call-start = ((), (), s32[]{:S(2)}) async-start(), calls=%async_computation.3 | async-start | bytes 2433024 | tf_op jit(solution)/shard_map/all_gather | solution.py:71
  77.9 73.0 %all-gather.7.cloned.1.call-start = ((), (), s32[]{:S(2)}) async-start(), calls=%async_computation.4 | async-start | bytes 1310720 | tf_op jit(solution)/shard_map/all_gather | solution.py:82
  135.5 90.2 %all-reduce.4.cloned.1.call-start = ((), (), s32[]{:S(2)}) async-start(), calls=%async_computation | async-start | bytes 532480 | tf_op jit(solution)/shard_map/psum | solution.py:93
  154.9 105.4 %all-reduce.6.cloned.1.call-start = ((), (), s32[]{:S(2)}) async-start(), calls=%async_computation.1 | async-start | bytes 532480 | tf_op jit(solution)/shard_map/psum | solution.py:114
  225.7 34.7 %copy-start.1 = (f32[520,128]{1,0:T(8,128)S(1)}, f32[520,128]{1,0:T(8,128)}, u32[]{:S(2)}) copy-start(f32[520,128]{1,0:T(8,128)} %all-reduce.4.cloned.1.call-done) | copy-start | bytes 798724
  229.6 107.8 %all-reduce.8.cloned.1.call-start = ((), (), s32[]{:S(2)}) async-start(), calls=%async_computation.2 | async-start | bytes 532480 | tf_op jit(solution)/shard_map/psum | solution.py:98
  260.4 85.2 %copy-start.2 = (f32[520,128]{1,0:T(8,128)S(1)}, f32[520,128]{1,0:T(8,128)}, u32[]{:S(2)}) copy-start(f32[520,128]{1,0:T(8,128)} %all-reduce.6.cloned.1.call-done) | copy-start | bytes 798724
Sparse Core Ops, SparseCore 0:
  78.0 52.6 all-gather.4
  135.6 15.2 all-gather.6
  155.0 70.5 all-reduce.3
  229.7 30.5 all-reduce.5
  265.9 71.4 all-reduce.7
